TPU v7x, 128 devices: a whole 4x4x4 slice. The times are simulated.
128 devices in a mesh: tok: 16 (over z, x_lo, core), col: 8 (over y, x_hi).
Axes of the slice: x: 4 (x_hi: 2, x_lo: 2; x = x_hi * 2 + x_lo), y: 4, z: 4, core: 2. Of those that a mesh axis runs over, the one named last changes fastest.
Arguments:
- tokens: bfloat16 [16384, 4096], P('tok'), may hold values from -6 to 6
- grads_out: bfloat16 [16384, 8192], P('tok', 'col'), may hold values from -0.046875 to 0.046875
- statistics: float32 [8, 16, 1024, 512], P('col', 'tok'), as said below
Outputs:
- update: bfloat16 [4096, 8192], P('tok', 'col')
- new_statistics: float32 [8, 16, 1024, 512], P('col', 'tok')
Inputs may be any that keep to these rules, and one draw needn't show every extreme that they name: statistics[j, (2 i + s) * 2 + w] holds columns w * 512 onward of a symmetric positive definite matrix with a positive diagonal.
All inputs are finite; a program needn't handle non-finite values.
Results may differ from a plain program's by a relative error of at most 0.007.
Values may be sent and summed in bfloat16 or wider, within the bound.
No kernel may reach another device: no remote copies, remote signals or barrier semaphores. Data moves between devices by JAX's collectives and lax.ppermute only.
A program may use at most 128 MiB of HBM per device.

v0:
```python
import math

import jax
import jax.numpy as jnp
from jax import lax
from jax.sharding import PartitionSpec as P

ITERS = 3


def swapped(block, axis, bit):
    count = lax.axis_size(axis)
    route = []
    for low in range(count):
        high = low | 1 << bit
        if high != low and high < count:
            route += [(low, high), (high, low)]
    return lax.ppermute(block, axis, route)


def doubling(values, levels, device, axis_dim, partner):
    for level_bit in range(levels):
        partner_part = partner(values, level_bit)
        low_side = device // 2**level_bit % 2 == 0
        values = jnp.where(
            low_side,
            jnp.concatenate([values, partner_part], axis_dim),
            jnp.concatenate([partner_part, values], axis_dim),
        )
    return values


def product(left_side, right_side):
    return jnp.einsum("bij,bjk->bik", left_side, right_side, precision=lax.Precision.HIGHEST)


def on_device(tokens, grads_out, statistics):
    device = lax.axis_index("tok")
    blocks = statistics.shape[0]
    order_size = statistics.shape[2]
    piece_width = statistics.shape[3]
    pieces = order_size // piece_width
    levels = pieces.bit_length() - 1
    rows_dev = tokens.shape[1] // lax.axis_size("tok")
    side_bit = device // pieces % 2
    column = device % pieces
    slab_index = device % (2 * pieces)

    def columns_of(values):
        return lax.dynamic_slice_in_dim(values, column * piece_width, piece_width, 2)

    owned = lax.psum_scatter(
        lax.dot_general(
            tokens, grads_out, (((0,), (0,)), ((), ())), preferred_element_type=jnp.float32
        ),
        "tok",
        scatter_dimension=0,
        tiled=True,
    ).astype(jnp.bfloat16)
    gradient = doubling(
        owned, levels + 1, device, 0, lambda portion, level_bit: swapped(portion, "tok", level_bit)
    )
    grad_cube = gradient.reshape(order_size, blocks, order_size)
    forward = jnp.transpose(grad_cube, (1, 0, 2))
    backward = jnp.transpose(grad_cube, (1, 2, 0))
    oriented = jnp.where(side_bit == 0, forward, backward)
    own_rows = lax.dynamic_slice_in_dim(oriented, column * piece_width, piece_width, 1)
    gram_piece = jnp.einsum("brc,bqc->brq", oriented, own_rows, preferred_element_type=jnp.float32)
    fresh_stat = statistics[:, 0] + gram_piece
    identity = jnp.eye(order_size, dtype=jnp.float32)

    def widen(values):
        return doubling(
            values, levels, device, 2, lambda portion, level_bit: swapped(portion, "tok", level_bit)
        )

    assembled = widen(fresh_stat)
    scaling = (2.5 / jnp.sqrt(jnp.sum(assembled * assembled, axis=(1, 2)) + 1e-06))[:, None, None]
    matrix = scaling * assembled
    factor = (5.0 * identity - matrix) * 0.25
    iterate = jnp.sqrt(jnp.sqrt(scaling)) * columns_of(factor)
    for repeat in range(1, ITERS):
        square = widen(product(factor, columns_of(factor)))
        fourth = widen(product(square, columns_of(square)))
        matrix = widen(product(fourth, columns_of(matrix)))
        factor = (5.0 * identity - matrix) * 0.25
        iterate = product(factor, iterate)
    own_root = doubling(
        iterate.astype(jnp.bfloat16),
        levels,
        device,
        2,
        lambda portion, level_bit: swapped(portion, "tok", level_bit),
    )
    other_root = swapped(own_root, "tok", levels)
    left_root = jnp.where(side_bit == 0, own_root, other_root)
    right_root = jnp.where(side_bit == 0, other_root, own_root)
    left_rows = lax.dynamic_slice_in_dim(left_root, slab_index * rows_dev, rows_dev, 1)
    mixed_rows = jnp.einsum(
        "bsr,rbc->bsc", left_rows, grad_cube, preferred_element_type=jnp.float32
    ).astype(jnp.bfloat16)
    update = jnp.einsum(
        "bsc,bcd->sbd", mixed_rows, right_root, preferred_element_type=jnp.float32
    ) * math.sqrt(order_size)
    return (update.reshape(rows_dev, blocks * order_size).astype(jnp.bfloat16), fresh_stat[:, None])


def solution(mesh):
    placed = (P("tok", None), P("tok", "col"), P("col", "tok", None, None))
    return jax.shard_map(
        on_device,
        mesh=mesh,
        in_specs=placed,
        out_specs=(P("tok", "col"), P("col", "tok", None, None)),
        check_vma=False,
    )
```

profile of v0, /device:TPU:1, one launch (start us, length us, event | category | flops | bytes accessed | tf_op | source)
XLA Modules:
  0.0 424.6 jit_solution(3885119850929868380)
XLA Ops:
  7.2 1.5 copy-done
  8.8 14.6 %fusion.164 = f32[4096,1024]{1,0:T(8,128)} fusion(bf16[1024,4096]{1,0:T(8,128)(2,1)} %param.3, bf16[1024,1024]{1,0:T(8,128)(2,1)S(1)} %copy-done), kind=kOutput, calls=%fused_computation.168 | convolution fusion | flops 8589934592 | bytes 27262976 | tf_op jit(solution)/shard_map/dot_general | solution.py:53
  23.4 184.0 %reduce-scatter.2.cloned.1.call-done = f32[256,1024]{1,0:T(8,128)} async-done(((f32[4096,1024]{1,0:T(8,128)}), f32[256,1024]{1,0:T(8,128)}) %reduce-scatter.2.cloned.1.call-update) | async-done | bytes 1048592 | tf_op jit(solution)/shard_map/reduce_scatter | solution.py:52
  208.7 2.6 collective-permute-start
  211.3 1.5 collective-permute-done
  213.5 2.9 copy.8
  216.9 20.9 %collective-permute-done.1 = bf16[512,1024]{1,0:T(8,128)(2,1)S(1)} collective-permute-done((bf16[512,1024]{1,0:T(8,128)(2,1)S(1)}, bf16[512,1024]{1,0:T(8,128)(2,1)S(1)}, u32[]{:S(2)}, u32[]{:S(2)}) %collective-permute-start.1) | collective-permute-done | bytes 1048608 | tf_op jit(solution)/shard_map/ppermute | solution.py:18
  237.8 1.4 copy.10
  239.2 5.5 %fusion.57 = bf16[1,1024,1024]{1,2,0:T(8,128)(2,1)S(1)} fusion(bf16[1,512,1024]{1,2,0:T(8,128)(2,1)} %copy.10, bf16[1,512,1024]{1,2,0:T(8,128)(2,1)S(1)} %copy.9, bf16[512,1,1024]{2,0,1:T(8,128)(2,1)S(1)} %bitcast.86, bf16[512,1,1024]{2,0,1:T(8,128)(2,1)S(1)} %bitcast.83, pred[]{:T(512)S(6)} %eq.58), kind=kLoop, calls=%fused_computation.74 | loop fusion | flops 19922944 | bytes 6291457 | tf_op jit(solution)/shard_map/jit(_where)/select_n | solution.py:66
  246.0 1.5 collective-permute-start.2
  247.5 2.5 fusion.43
  252.6 1.7 multiply_reduce_fusion
  255.1 3.1 fusion.44
  259.1 7.4 %fusion.1 = f32[1024,512]{0,1:T(8,128)S(1)} fusion(f32[1024,512]{0,1:T(8,128)S(1)} %bitcast.84, f32[1024,512]{0,1:T(8,128)S(1)} %bitcast_add_fusion, f32[]{:T(128)S(6)} %div.24, pred[]{:T(512)S(6)} %eq.59, f32[1,1024,1024]{1,2,0:T(8,128)S(1)} %fusion.44, s32[]{:T(128)S(6)} %select_n.257, f32[1,1024,1024]{1,2,0:T(8,128)S(1)} %copy-done.4), kind=kOutput, calls=%fused_computation.4 | convolution fusion | flops 6451888128 | bytes 10485769 | tf_op jit(solution)/shard_map/bij,bjk->bik/dot_general | solution.py:34
  267.2 3.8 collective-permute-done.3
  271.0 7.6 %fusion.14 = f32[1024,512]{0,1:T(8,128)S(1)} fusion(f32[1024,512]{0,1:T(8,128)S(1)} %bitcast.98, f32[1024,512]{0,1:T(8,128)S(1)} %fusion.1, s32[]{:T(128)S(6)} %select_n.257, f32[1,1024,512]{1,2,0:T(8,128)S(1)} %collective-permute-done.3, f32[1,1024,512]{1,2,0:T(8,128)S(1)} %bitcast.94, pred[]{:T(512)S(6)} %eq.59), kind=kOutput, calls=%fused_computation.17 | convolution fusion | flops 6447169536 | bytes 10487296 | tf_op jit(solution)/shard_map/bij,bjk->bik/dot_general | solution.py:34
  279.5 3.8 collective-permute-done.4
  283.3 7.0 %fusion.20 = f32[1024,512]{0,1:T(8,128)S(1)} fusion(f32[1024,512]{0,1:T(8,128)S(1)} %bitcast.99, f32[1024,512]{0,1:T(8,128)S(1)} %fusion.14, pred[]{:T(512)S(6)} %eq.59, f32[1,1024,1024]{1,2,0:T(8,128)S(1)} %fusion.44, s32[]{:T(128)S(6)} %select_n.257), kind=kOutput, calls=%fused_computation.28 | convolution fusion | flops 6445596672 | bytes 8388613 | tf_op jit(solution)/shard_map/bij,bjk->bik/dot_general | solution.py:34
  290.9 3.8 collective-permute-done.5
  296.3 7.2 %fusion.70 = f32[1024,512]{0,1:T(8,128)S(1)} fusion(f32[1,1024,1024]{1,2,0:T(8,128)S(1)} %maximum_select_fusion.7, s32[]{:T(128)S(6)} %select_n.257, f32[1,1024,1024]{1,2,0:T(8,128)S(1)} %copy-done.4, f32[1024,512]{0,1:T(8,128)S(1)} %bitcast.89, f32[1024,512]{0,1:T(8,128)S(1)} %fusion.20, pred[]{:T(512)S(6)} %eq.59), kind=kOutput, calls=%fused_computation.90 | convolution fusion | flops 6450839552 | bytes 10485765 | tf_op jit(solution)/shard_map/bij,bjk->bik/dot_general | solution.py:34
  304.2 3.8 collective-permute-done.6
  308.0 7.6 %fusion.26 = f32[1024,512]{0,1:T(8,128)S(1)} fusion(f32[1024,512]{0,1:T(8,128)S(1)} %bitcast.100, f32[1024,512]{0,1:T(8,128)S(1)} %fusion.70, s32[]{:T(128)S(6)} %select_n.257, f32[1,1024,512]{1,2,0:T(8,128)S(1)} %collective-permute-done.6, f32[1,1024,512]{1,2,0:T(8,128)S(1)} %bitcast.96, pred[]{:T(512)S(6)} %eq.59), kind=kOutput, calls=%fused_computation.37 | convolution fusion | flops 6447169536 | bytes 10487296 | tf_op jit(solution)/shard_map/bij,bjk->bik/dot_general | solution.py:34
  316.3 3.8 collective-permute-done.7
  320.0 8.4 %fusion.32 = f32[1024,512]{0,1:T(8,128)} fusion(f32[1024,512]{0,1:T(8,128)S(1)} %bitcast.97, f32[1024,512]{0,1:T(8,128)S(1)} %fusion.26, pred[]{:T(512)S(6)} %eq.59, f32[1,1024,1024]{1,2,0:T(8,128)S(1)} %maximum_select_fusion.7, s32[]{:T(128)S(6)} %select_n.257), kind=kOutput, calls=%fused_computation.48 | convolution fusion | flops 6445596672 | bytes 8388613 | tf_op jit(solution)/shard_map/bij,bjk->bik/dot_general | solution.py:34
  329.2 17.7 %fusion.67 = f32[1024,512]{1,0:T(8,128)S(1)} fusion(f32[1024,512]{0,1:T(8,128)} %bitcast.90, f32[1024,512]{0,1:T(8,128)} %copy-done.8, pred[]{:T(512)S(6)} %eq.59, f32[]{:T(128)S(6)} %sqrt.18, f32[1,1024,1024]{1,2,0:T(8,128)} %copy-done.5, s32[]{:T(128)S(6)} %select_n.257, f32[1,1024,1024]{1,2,0:T(8,128)} %fusion.43), kind=kOutput, calls=%fused_computation.87 | convolution fusion | flops 6451363840 | bytes 10485769 | tf_op jit(solution)/shard_map/bij,bjk->bik/dot_general | solution.py:34
  346.9 10.5 %fusion.106 = bf16[1,1024,512]{1,2,0:T(8,128)(2,1)S(1)} fusion(f32[1024,512]{1,0:T(8,128)S(1)} %fusion.67, f32[1024,512]{0,1:T(8,128)} %bitcast.27, f32[1024,512]{0,1:T(8,128)} %fusion.32, pred[]{:T(512)S(6)} %eq.59), kind=kOutput, calls=%fused_computation.122 | convolution fusion | flops 6450315264 | bytes 7340033 | tf_op jit(solution)/shard_map/bij,bjk->bik/dot_general | solution.py:34
  357.9 2.5 collective-permute-done.9
  360.5 2.3 maximum_select_fusion.16
  362.8 1.8 copy.14
  364.6 45.6 %collective-permute-done.10 = bf16[1,1024,1024]{1,2,0:T(8,128)(2,1)} collective-permute-done((bf16[1,1024,1024]{1,2,0:T(8,128)(2,1)}, bf16[1,1024,1024]{1,2,0:T(8,128)(2,1)}, u32[]{:S(2)}, u32[]{:S(2)}) %collective-permute-start.10) | collective-permute-done | bytes 2097184 | tf_op jit(solution)/shard_map/ppermute | solution.py:18
  410.2 5.0 %fusion.116 = bf16[256,1024]{0,1:T(8,128)(2,1)} fusion(bf16[1,1024,1024]{1,2,0:T(8,128)(2,1)} %collective-permute-done.10, bf16[1,1024,1024]{1,2,0:T(8,128)(2,1)} %maximum_select_fusion.16, pred[]{:T(512)S(6)} %eq.58, bf16[512,1024]{1,0:T(8,128)(2,1)} %copy-done.6, bf16[512,1024]{1,0:T(8,128)(2,1)S(1)} %maximum_select_fusion.21, s32[]{:T(128)S(6)} %select_n.273), kind=kOutput, calls=%fused_computation.126 | convolution fusion | flops 1085276160 | bytes 7866368 | tf_op jit(solution)/shard_map/bsc,bcd->sbd/dot_general | solution.py:102
  415.2 2.0 copy.13
  (37 shorter events, 13.7 us)
Async XLA Ops:
  7.2 1.6 copy-start
  7.2 200.2 %reduce-scatter.2.cloned.1.call-start = ((), (), s32[]{:S(2)}) async-start(), calls=%async_computation.1 | async-start | bytes 17825792 | tf_op jit(solution)/shard_map/reduce_scatter | solution.py:52
  208.7 4.2 collective-permute-start
  213.4 24.5 %collective-permute-start.1 = (bf16[512,1024]{1,0:T(8,128)(2,1)S(1)}, bf16[512,1024]{1,0:T(8,128)(2,1)S(1)}, u32[]{:S(2)}, u32[]{:S(2)}) collective-permute-start(bf16[512,1024]{1,0:T(8,128)(2,1)S(1)} %maximum_select_fusion.21), channel_id=1, source_target_pairs={{0,16},{16,0},{8,24},{24,8},{32,48},{48,32},{40,56},{56,40},{64,80... | collective-permute-start | bytes 3145736 | tf_op jit(solution)/shard_map/ppermute | solution.py:18
  237.8 1.4 copy-start.6
  239.2 5.5 %copy-start.7 = (f32[1,1,1024,512]{2,3,1,0:T(8,128)S(1)}, f32[1,1,1024,512]{2,3,1,0:T(8,128)}, u32[]{:S(2)}) copy-start(f32[1,1,1024,512]{2,3,1,0:T(8,128)} %copy.8) | copy-start | bytes 6291460
  246.0 5.3 %collective-permute-start.2 = (f32[1,1024,512]{1,2,0:T(8,128)S(1)}, f32[1,1024,512]{1,2,0:T(8,128)S(1)}, u32[]{:S(2)}, u32[]{:S(2)}) collective-permute-start(f32[1,1024,512]{1,2,0:T(8,128)S(1)} %bitcast.78), channel_id=1, source_target_pairs={{0,8},{8,0},{16,24},{24,16},{32,40},{40,32},{48,56},{56,48},{64,72... | collective-permute-start | bytes 6291464 | tf_op jit(solution)/shard_map/ppermute | solution.py:18
  251.3 1.3 copy-start.2
  255.0 3.2 copy-start.3
  255.0 4.1 copy-start.4
  258.2 25.1 %copy-start.5 = (f32[1,1024,1024]{1,2,0:T(8,128)}, f32[1,1024,1024]{1,2,0:T(8,128)S(1)}, u32[]{:S(2)}) copy-start(f32[1,1024,1024]{1,2,0:T(8,128)S(1)} %fusion.44) | copy-start | bytes 12582916
  266.5 4.5 %collective-permute-start.3 = (f32[1,1024,512]{1,2,0:T(8,128)S(1)}, f32[1,1024,512]{1,2,0:T(8,128)S(1)}, u32[]{:S(2)}, u32[]{:S(2)}) collective-permute-start(f32[1,1024,512]{1,2,0:T(8,128)S(1)} %bitcast.93), channel_id=1, source_target_pairs={{0,8},{8,0},{16,24},{24,16},{32,40},{40,32},{48,56},{56,48},{64,72... | collective-permute-start | bytes 6291464 | tf_op jit(solution)/shard_map/ppermute | solution.py:18
  278.6 4.7 %collective-permute-start.4 = (f32[1,1024,512]{1,2,0:T(8,128)S(1)}, f32[1,1024,512]{1,2,0:T(8,128)S(1)}, u32[]{:S(2)}, u32[]{:S(2)}) collective-permute-start(f32[1,1024,512]{1,2,0:T(8,128)S(1)} %bitcast.92), channel_id=1, source_target_pairs={{0,8},{8,0},{16,24},{24,16},{32,40},{40,32},{48,56},{56,48},{64,72... | collective-permute-start | bytes 6291464 | tf_op jit(solution)/shard_map/ppermute | solution.py:18
  290.3 5.3 %copy-start.8 = (f32[1024,512]{0,1:T(8,128)}, f32[1024,512]{0,1:T(8,128)S(1)}, u32[]{:S(2)}) copy-start(f32[1024,512]{0,1:T(8,128)S(1)} %fusion.20) | copy-start | bytes 6291460
  290.3 4.4 %collective-permute-start.5 = (f32[1,1024,512]{1,2,0:T(8,128)S(1)}, f32[1,1024,512]{1,2,0:T(8,128)S(1)}, u32[]{:S(2)}, u32[]{:S(2)}) collective-permute-start(f32[1,1024,512]{1,2,0:T(8,128)S(1)} %bitcast.87), channel_id=1, source_target_pairs={{0,8},{8,0},{16,24},{24,16},{32,40},{40,32},{48,56},{56,48},{64,72... | collective-permute-start | bytes 6291464 | tf_op jit(solution)/shard_map/ppermute | solution.py:18
  294.7 1.6 copy-start.9
  303.5 4.5 %collective-permute-start.6 = (f32[1,1024,512]{1,2,0:T(8,128)S(1)}, f32[1,1024,512]{1,2,0:T(8,128)S(1)}, u32[]{:S(2)}, u32[]{:S(2)}) collective-permute-start(f32[1,1024,512]{1,2,0:T(8,128)S(1)} %bitcast.95), channel_id=1, source_target_pairs={{0,8},{8,0},{16,24},{24,16},{32,40},{40,32},{48,56},{56,48},{64,72... | collective-permute-start | bytes 6291464 | tf_op jit(solution)/shard_map/ppermute | solution.py:18
  315.6 4.5 %collective-permute-start.7 = (f32[1,1024,512]{1,2,0:T(8,128)S(1)}, f32[1,1024,512]{1,2,0:T(8,128)S(1)}, u32[]{:S(2)}, u32[]{:S(2)}) collective-permute-start(f32[1,1024,512]{1,2,0:T(8,128)S(1)} %bitcast.91), channel_id=1, source_target_pairs={{0,8},{8,0},{16,24},{24,16},{32,40},{40,32},{48,56},{56,48},{64,72... | collective-permute-start | bytes 6291464 | tf_op jit(solution)/shard_map/ppermute | solution.py:18
  328.4 18.4 %collective-permute-start.8 = (f32[1,1024,512]{1,2,0:T(8,128)}, f32[1,1024,512]{1,2,0:T(8,128)}, u32[]{:S(2)}, u32[]{:S(2)}) collective-permute-start(f32[1,1024,512]{1,2,0:T(8,128)} %bitcast.26), channel_id=1, source_target_pairs={{0,8},{8,0},{16,24},{24,16},{32,40},{40,32},{48,56},{56,48},{64,72... | collective-permute-start | bytes 6291464 | tf_op jit(solution)/shard_map/ppermute | solution.py:18
  357.4 3.1 collective-permute-start.9
  362.8 47.4 %collective-permute-start.10 = (bf16[1,1024,1024]{1,2,0:T(8,128)(2,1)}, bf16[1,1024,1024]{1,2,0:T(8,128)(2,1)}, u32[]{:S(2)}, u32[]{:S(2)}) collective-permute-start(bf16[1,1024,1024]{1,2,0:T(8,128)(2,1)} %maximum_select_fusion.16), channel_id=1, source_target_pairs={{0,16},{16,0},{8,24},{24,8},{32,48},{48,32},{40,56},{56,40},{64,80... | collective-permute-start | bytes 6291464 | tf_op jit(solution)/shard_map/ppermute | solution.py:18
  410.2 7.0 %copy-start.1 = (bf16[1024,1024]{1,0:T(8,128)(2,1)S(1)}, bf16[1024,1024]{1,0:T(8,128)(2,1)}, u32[]{:S(2)}) copy-start(bf16[1024,1024]{1,0:T(8,128)(2,1)} %param.4) | copy-start | bytes 6291460
Sparse Core Ops, SparseCore 0:
  23.5 183.8 reduce-scatter.1
where the time goes:
time: 432 us; the launch traced here: 425 us
  waiting for transfers between devices  275 us (64%)
  matrix products  94.2 us (22%)
  other arithmetic  17.8 us (4%)
  between operations  15.6 us (4%)
  local copies, waits for them, and re-layouts  13.1 us (3%)
  starting transfers between devices  9.08 us (2%)
    reduce_scatter x1, waiting for transfers between devices, on_device(): lax.psum_scatter(lax.dot_general(tokens, grads_out, (((0,), (0,)), ((), (...  184 us
    ppermute x11, waiting for transfers between devices, swapped(): return lax.ppermute(block, axis, route)  90.8 us
    dot_general x8, matrix products, product(): jnp.einsum('bij,bjk->bik', left_side, right_side, precision=lax.Precision...  73.3 us
    dot_general x1, matrix products, on_device(): lax.dot_general(tokens, grads_out, (((0,), (0,)), ((), ())), preferred_el...  14.6 us
    unnamed x23, local copies, waits for them, and re-layouts  11.2 us
    ppermute x11, starting transfers between devices, swapped(): return lax.ppermute(block, axis, route)  9.04 us
  transfers between devices with their start and end apart: 12, of which 11 were waited for; matrix products, arithmetic and copies ran while one was open for 6% of the time, Pallas kernels for 0%

commit v1 on v0

v1 whole, which is shorter than its diff:
```python
import functools
import math

import jax
import jax.numpy as jnp
from jax import lax
from jax.experimental import pallas as pl
from jax.experimental.pallas import tpu as pltpu
from jax.sharding import PartitionSpec as P

CHUNKS = (384, 352, 288)
EFFORT = 4


def swapped(block, axis, bit):
    count = lax.axis_size(axis)
    route = []
    for low in range(count):
        high = low | 1 << bit
        if high != low and high < count:
            route += [(low, high), (high, low)]
    return lax.ppermute(block, axis, route)


def ring_sent(block, axis, stride):
    count = lax.axis_size(axis)
    route = []
    for source in range(count):
        step = stride if source % 2 == 0 else -stride
        route.append((source, (source + step) % count))
    return lax.ppermute(block, axis, route)


def regrouped(block, moves):
    route = []
    for base in range(0, lax.axis_size("tok"), 4):
        route += [(base + source, base + target) for source, target in moves]
    return lax.ppermute(block, "tok", route)


def after(value, *events):
    return lax.optimization_barrier((value, *events))[0]


def partial_kernel(kinds, place_ref, *refs):
    count = len(kinds)
    for index, kind in enumerate(kinds):
        picked, grads, partial = refs[index], refs[count + index], refs[2 * count + index]
        partial[...] = matmul(picked[...], grads[...], (0, 0)).astype(kind)


def partial_products(place, tokens, grads_out, blocks, effort):
    order = grads_out.shape[1]
    half = order // 2
    depth = tokens.shape[0]
    tile = 256
    steps = order // tile
    kinds = [jnp.float32 if owner == 0 else jnp.bfloat16 for _, owner in blocks]
    picked = [
        pl.BlockSpec((depth, tile), lambda step, place, where=where: (0, place[where] * steps + step))
        for where, _ in blocks
    ]
    columns = [
        pl.BlockSpec((depth, half), lambda step, place, owner=owner: (0, place[owner])) for _, owner in blocks
    ]
    return pl.pallas_call(
        functools.partial(partial_kernel, kinds),
        out_shape=[jax.ShapeDtypeStruct((order, half), kind) for kind in kinds],
        grid_spec=pltpu.PrefetchScalarGridSpec(
            num_scalar_prefetch=1,
            grid=(steps,),
            in_specs=picked + columns,
            out_specs=[pl.BlockSpec((tile, half), lambda step, place: (step, 0)) for _ in blocks],
        ),
        compiler_params=pltpu.CompilerParams(vmem_limit_bytes=12 << 20),
        cost_estimate=pl.CostEstimate(
            flops=effort * 2 * len(blocks) * order * half * depth,
            bytes_accessed=effort * 6 * len(blocks) * order * half,
            transcendentals=0,
        ),
        name="partial",
    )(place, *[tokens] * len(blocks), *[grads_out] * len(blocks))


def places(device):
    ring = lax.axis_size("tok") // 4
    core = device % 2
    at = device // 4
    turn = 1 - 2 * core
    return jnp.stack(
        [core, 1 - core, (at + turn) % ring, (at - turn) % ring, (at + 2) % ring, at, device // 2 % 2]
    ).astype(jnp.int32)


def block_of_gradient(place, tokens, grads_out, piece, device):
    stride = 4
    starts = [sum(CHUNKS[:index]) for index in range(len(CHUNKS))]
    ahead, behind, across, home = 2, 3, 4, 5
    own, mate = 0, 1
    (given,) = partial_products(place, tokens, grads_out, [(ahead, mate)], 1)
    received = swapped(given, "tok", 0)
    piece = after(piece, given).astype(jnp.bfloat16)
    first = regrouped(piece, [(0, 2), (3, 1), (1, 0), (2, 3)])
    second = regrouped(after(piece, first), [(1, 2), (2, 1)])
    (local,) = partial_products(after(place, given), tokens, grads_out, [(behind, own)], 1)
    totals = [None] * len(CHUNKS)

    def joined(*terms):
        total = terms[0].astype(jnp.float32)
        for term in terms[1:]:
            total = total + term.astype(jnp.float32)
        return total.astype(jnp.bfloat16)

    for k, (start, size) in enumerate(zip(starts, CHUNKS)):
        totals[k] = joined(local[start : start + size], received[start : start + size])
    events = totals
    for hop, (own_block, mate_block) in enumerate(((across, across), (ahead, behind), (home, home))):
        given, local = partial_products(
            after(place, *events), tokens, grads_out, [(mate_block, mate), (own_block, own)], EFFORT
        )
        events = [given, first] if hop == 1 else [given]
        received = swapped(given, "tok", 0)
        for k, (start, size) in enumerate(zip(starts, CHUNKS)):
            arrived = ring_sent(totals[k], "tok", stride)
            if hop == 1 and k == len(CHUNKS) - 1:
                arrived = after(arrived, second)
            totals[k] = joined(local[start : start + size], received[start : start + size], arrived)
    own_chunks = [joined(total, swapped(total, "tok", 1)) for total in totals]
    mate_chunks = [swapped(chunk, "tok", 0) for chunk in own_chunks]
    spot = device % 4
    second = jnp.where((spot == 0) | (spot == 3), piece, second)
    low = jnp.where(spot < 2, second, first)
    high = jnp.where(spot < 2, first, second)
    return own_chunks, mate_chunks, low, high


def iterate_terms():
    terms = [25.0 / 16.0, -5.0 / 16.0, 0.0, 0.0, 0.0, 0.0, 0.0]
    for power in range(6):
        terms[power + 1] -= 0.25 * math.comb(5, power) * 1.25 ** (5 - power) * (-0.25) ** power
    return terms


def matmul(left_side, right_side, contract):
    return lax.dot_general(
        left_side, right_side, ((contract[:1], contract[1:]), ((), ())),
        preferred_element_type=jnp.float32,
    )


TILE = 256


def root_kernel(place_ref, *refs):
    count = len(CHUNKS)
    chunks = refs[: 2 * count]
    low_ref, high_ref, root_ref, own_ref, mate_ref = refs[2 * count : 2 * count + 5]
    stat, work, extra, mat_b, pow_b, cube_b, mix_b = refs[2 * count + 5 :]
    order, half = own_ref.shape
    core = place_ref[0]
    for index, chunk in enumerate(chunks):
        start = sum(CHUNKS[: index % count])
        whole = own_ref if index < count else mate_ref
        whole[pl.ds(start, chunk.shape[0]), :] = chunk[...]
    terms = iterate_terms()
    tiles = [pl.ds(start, TILE) for start in range(0, order, TILE)]

    @pl.when(core == 0)
    def _():
        for tile in tiles:
            gram = matmul(own_ref[tile, :], own_ref[...], (1, 1))
            gram += matmul(mate_ref[tile, :], mate_ref[...], (1, 1))
            stat[tile, :half] = gram[:, :half] + low_ref[tile, :].astype(jnp.float32)
            stat[tile, half:] = gram[:, half:] + high_ref[tile, :].astype(jnp.float32)

    @pl.when(core == 1)
    def _():
        for tile in tiles:
            rows_of = mate_ref if tile.start < half else own_ref
            picked = rows_of[:, pl.ds(tile.start % half, TILE)]
            stat[tile, :half] = matmul(picked, mate_ref[...], (0, 0)) + low_ref[tile, :].astype(jnp.float32)
            stat[tile, half:] = matmul(picked, own_ref[...], (0, 0)) + high_ref[tile, :].astype(jnp.float32)

    total = jnp.zeros((1, order), jnp.float32)
    for tile in tiles:
        values = stat[tile, :]
        total += jnp.sum(values * values, axis=0, keepdims=True)
    total = jnp.sum(total, axis=1, keepdims=True)
    zeta = 2.5 * lax.rsqrt(total + 1e-06)
    for tile in tiles:
        matrix = zeta * stat[tile, :]
        stat[tile, :] = matrix
        mat_b[tile, :] = matrix.astype(jnp.bfloat16)
    for tile in tiles:
        second = matmul(mat_b[tile, :], mat_b[...], (1, 0))
        work[tile, :] = second
        pow_b[tile, :] = second.astype(jnp.bfloat16)
    for tile in tiles:
        third = matmul(mat_b[tile, :], pow_b[...], (1, 0))
        cube_b[tile, :] = third.astype(jnp.bfloat16)
        second = work[tile, :]
        matrix = stat[tile, :]
        mix_b[tile, :] = (terms[6] * third + terms[5] * second + terms[4] * matrix).astype(jnp.bfloat16)
        work[tile, :] = terms[3] * third + terms[2] * second + terms[1] * matrix
    ident = terms[0]
    for tile in tiles:
        rest = work[tile, :] + matmul(mix_b[tile, :], cube_b[...], (1, 0))
        work[tile, :] = rest
        pow_b[tile, :] = rest.astype(jnp.bfloat16)
    for tile in tiles:
        square = matmul(pow_b[tile, :], pow_b[...], (1, 0)) + (2.0 * ident) * work[tile, :]
        mix_b[tile, :] = square.astype(jnp.bfloat16)
    for tile in tiles:
        value = matmul(mat_b[tile, :], mix_b[...], (1, 0)) + (ident * ident) * stat[tile, :]
        extra[tile, :] = value
        cube_b[tile, :] = value.astype(jnp.bfloat16)
    for tile in tiles:
        later = matmul(cube_b[tile, :], mix_b[...], (1, 0)) + (ident * ident) * extra[tile, :]
        mat_b[tile, :] = later.astype(jnp.bfloat16)
        work[tile, :] = 1.25 * work[tile, :] - (0.25 * ident) * later
    scale = jnp.sqrt(jnp.sqrt(zeta))
    for tile in tiles:
        row = lax.broadcasted_iota(jnp.int32, (TILE, order), 0) + tile.start
        column = lax.broadcasted_iota(jnp.int32, (TILE, order), 1)
        rest = work[tile, :] - 0.25 * matmul(pow_b[tile, :], mat_b[...], (1, 0))
        rest = rest + jnp.where(row == column, 1.25 * ident, 0.0)
        root_ref[tile, :] = (scale * rest).astype(jnp.bfloat16)


def stat_kernel(place_ref, own_ref, mate_ref, old_ref, fresh_ref):
    order, half = own_ref.shape
    core = place_ref[0]
    left_chip = place_ref[6]

    @pl.when(left_chip == 0)
    def _():
        picked = pl.ds(pl.multiple_of(core * half, half), half)
        own_rows = own_ref[picked, :]
        mate_rows = mate_ref[picked, :]
        for start in range(0, order, TILE):
            tile = pl.ds(start, TILE)
            gram = matmul(own_ref[tile, :], own_rows, (1, 1)) + matmul(mate_ref[tile, :], mate_rows, (1, 1))
            fresh_ref[tile, :] = old_ref[tile, :] + gram

    @pl.when(left_chip == 1)
    def _():
        own_at = pl.multiple_of(core * half, half)
        mate_at = pl.multiple_of((1 - core) * half, half)
        for start in range(0, half, TILE):
            for rows_of, at in ((own_ref, own_at), (mate_ref, mate_at)):
                tile = pl.ds(at + start, TILE)
                gram = matmul(rows_of[:, pl.ds(start, TILE)], own_ref[...], (0, 0))
                fresh_ref[tile, :] = old_ref[tile, :] + gram


def update_kernel(place_ref, own_ref, mate_ref, own_root_ref, mate_root_ref, update_ref):
    order, half = own_ref.shape
    rows = update_ref.shape[0]
    core = place_ref[0]
    slab = pl.ds(pl.multiple_of((2 * place_ref[6] + core) * rows, rows), rows)

    def finish(first, second, left, right):
        left_rows = left[slab, :]
        mixed_first = matmul(left_rows, first[...], (1, 0)).astype(jnp.bfloat16)
        mixed_second = matmul(left_rows, second[...], (1, 0)).astype(jnp.bfloat16)
        update = matmul(mixed_first, right[:half, :], (1, 0)) + matmul(mixed_second, right[half:, :], (1, 0))
        update_ref[...] = (update * math.sqrt(order)).astype(jnp.bfloat16)

    @pl.when(core == 0)
    def _():
        finish(own_ref, mate_ref, own_root_ref, mate_root_ref)

    @pl.when(core == 1)
    def _():
        finish(mate_ref, own_ref, mate_root_ref, own_root_ref)


VMEM = pl.BlockSpec(memory_space=pltpu.VMEM)
SMEM = pl.BlockSpec(memory_space=pltpu.SMEM)


def on_device(tokens, grads_out, statistics):
    device = lax.axis_index("tok")
    order = statistics.shape[2]
    half = statistics.shape[3]
    rows_dev = tokens.shape[1] // lax.axis_size("tok")
    piece = statistics[0, 0]
    place = places(device)
    tokens = pltpu.with_memory_space_constraint(tokens, pltpu.HBM)
    grads_out = pltpu.with_memory_space_constraint(grads_out, pltpu.HBM)
    own_chunks, mate_chunks, low, high = block_of_gradient(place, tokens, grads_out, piece, device)
    wide = (order, order)
    halves = jax.ShapeDtypeStruct((order, half), jnp.bfloat16)
    own_root, own_half, mate_half = pl.pallas_call(
        root_kernel,
        out_shape=(jax.ShapeDtypeStruct(wide, jnp.bfloat16), halves, halves),
        in_specs=[SMEM] + [VMEM] * (2 * len(CHUNKS) + 2),
        out_specs=(VMEM, VMEM, VMEM),
        scratch_shapes=[pltpu.VMEM(wide, jnp.float32)] * 3 + [pltpu.VMEM(wide, jnp.bfloat16)] * 4,
        compiler_params=pltpu.CompilerParams(vmem_limit_bytes=44 << 20),
        cost_estimate=pl.CostEstimate(flops=16 * order**3, bytes_accessed=8 * order**2, transcendentals=0),
        name="root",
    )(place, *own_chunks, *mate_chunks, low, high)
    mate_root = swapped(own_root, "tok", 0)
    fresh_stat = pl.pallas_call(
        stat_kernel,
        out_shape=jax.ShapeDtypeStruct((order, half), jnp.float32),
        in_specs=[SMEM, VMEM, VMEM, VMEM],
        out_specs=VMEM,
        compiler_params=pltpu.CompilerParams(vmem_limit_bytes=20 << 20),
        cost_estimate=pl.CostEstimate(flops=order**3, bytes_accessed=6 * order**2, transcendentals=0),
        name="statistics",
    )(place, own_half, mate_half, piece)
    update = pl.pallas_call(
        update_kernel,
        out_shape=jax.ShapeDtypeStruct((rows_dev, order), jnp.bfloat16),
        in_specs=[SMEM, VMEM, VMEM, VMEM, VMEM],
        out_specs=VMEM,
        compiler_params=pltpu.CompilerParams(vmem_limit_bytes=20 << 20),
        cost_estimate=pl.CostEstimate(flops=order**3, bytes_accessed=8 * order**2, transcendentals=0),
        name="update",
    )(place, own_half, mate_half, own_root, mate_root)
    return update, fresh_stat[None, None]


def solution(mesh):
    placed = (P("tok", None), P("tok", "col"), P("col", "tok", None, None))
    return jax.shard_map(
        on_device,
        mesh=mesh,
        in_specs=placed,
        out_specs=(P("tok", "col"), P("col", "tok", None, None)),
        check_vma=False,
    )
```

time: 432 us -> 120 us (0.28); the launches traced: 425 us -> 119 us
  waiting for transfers between devices: 275 us -> 15.2 us
  matrix products: 94.2 us -> 0 us
  Pallas kernels: 0 us -> 53.6 us
  starting transfers between devices: 9.08 us -> 41.6 us
  between operations: 15.6 us -> 0.92 us
  local copies, waits for them, and re-layouts: 13.1 us -> 0.09 us
  other arithmetic: 17.8 us -> 7.73 us
    reduce_scatter x1 -> x0, waiting for transfers between devices: 184 us -> none  [on_device(): lax.psum_scatter(lax.dot_general(tokens, grads_out, (((0,), (0,)), ((), (...]
    dot_general x11 -> x0, matrix products: 94.2 us -> none  [the longest x8 73.3 us: product(): jnp.einsum('bij,bjk->bik', left_side, right_side, precision=lax.Precision...]
    ppermute x11, waiting for transfers between devices: 90.8 us -> 2.22 us  [swapped(): return lax.ppermute(block, axis, route)]
    pallas_call x0 -> x8, Pallas kernels: none -> 53.6 us  [the longest x5 27.1 us: partial_products(): pl.pallas_call(functools.partial(partial_kernel, kinds), out_shape=[jax.S...]
    ppermute x0 -> x11, starting transfers between devices: none -> 16.7 us  [the longest x9 14.4 us: ring_sent(): return lax.ppermute(block, axis, route)]
    ppermute x11, starting transfers between devices: 9.04 us -> 24.9 us  [swapped(): return lax.ppermute(block, axis, route)]
    ppermute x0 -> x11, waiting for transfers between devices: none -> 13 us  [the longest x9 13 us: ring_sent(): return lax.ppermute(block, axis, route)]
    unnamed x23 -> x2, local copies, waits for them, and re-layouts: 11.2 us -> 0.01 us
  transfers between devices with their start and end apart: 12 -> 22, of which waited for: 11 -> 10; matrix products, arithmetic and copies ran while one was open for 6% -> 6% of each run, Pallas kernels for 0% -> 22%
where the time goes in v1:
time: 120 us; the launch traced here: 119 us
  Pallas kernels  53.6 us (45%)
  starting transfers between devices  41.6 us (35%)
  waiting for transfers between devices  15.2 us (13%)
  other arithmetic  7.73 us (6%)
    pallas_call x5, Pallas kernels, partial_products(): pl.pallas_call(functools.partial(partial_kernel, kinds), out_shape=[jax.S...  27.1 us
    ppermute x11, starting transfers between devices, swapped(): return lax.ppermute(block, axis, route)  24.9 us
    pallas_call x1, Pallas kernels, on_device(): pl.pallas_call(root_kernel, out_shape=(jax.ShapeDtypeStruct(wide, jnp.bfl...  20.6 us
    ppermute x9, starting transfers between devices, ring_sent(): return lax.ppermute(block, axis, route)  14.4 us
    ppermute x9, waiting for transfers between devices, ring_sent(): return lax.ppermute(block, axis, route)  13 us
    convert_element_type x15, other arithmetic, joined(): return total.astype(jnp.bfloat16)  5.12 us
    pallas_call x1, Pallas kernels, on_device(): pl.pallas_call(stat_kernel, out_shape=jax.ShapeDtypeStruct((order, half),...  3.2 us
    pallas_call x1, Pallas kernels, on_device(): pl.pallas_call(update_kernel, out_shape=jax.ShapeDtypeStruct((rows_dev, o...  2.69 us
  transfers between devices with their start and end apart: 22, of which 10 were waited for; matrix products, arithmetic and copies ran while one was open for 6% of the time, Pallas kernels for 22%

profile of v1, /device:TPU:1, one launch (start us, length us, event | category | flops | bytes accessed | tf_op | source)
XLA Modules:
  0.0 119.0 jit_solution(17748025870033443690)
XLA Ops:
  0.8 4.5 %partial.5 = bf16[1024,512]{1,0:T(8,128)(2,1)S(1)} custom-call(s32[7]{0:T(128)S(1)} %stack.31.place_ref, bf16[1024,4096]{1,0:T(8,128)(2,1)} %refs_1_.9, bf16[1024,1024]{1,0:T(8,128)(2,1)} %refs_3_.5), custom_call_target="tpu_custom_call" | custom-call | flops 1073741824 | bytes 3145728 | tf_op jit(solution)/shard_map/partial/pallas_call | solution.py:66
  5.4 1.5 %collective-permute-start = (bf16[1024,512]{1,0:T(8,128)(2,1)S(1)}, bf16[1024,512]{1,0:T(8,128)(2,1)}, u32[]{:S(2)}, u32[]{:S(2)}) collective-permute-start(bf16[1024,512]{1,0:T(8,128)(2,1)S(1)} %partial.5), channel_id=1, source_target_pairs={{0,8},{8,0},{16,24},{24,16},{32,40},{40,32},{48,56},{56,48},{64,72... | collective-permute-start | bytes 3145736 | tf_op jit(solution)/shard_map/ppermute | solution.py:22
  8.0 4.5 %partial.6 = f32[1024,512]{1,0:T(8,128)S(1)} custom-call(s32[7]{0:T(128)S(1)} %stack.31.place_ref, bf16[1024,4096]{1,0:T(8,128)(2,1)} %refs_1_.9, bf16[1024,1024]{1,0:T(8,128)(2,1)} %refs_3_.5), custom_call_target="tpu_custom_call" | custom-call | flops 1073741824 | bytes 3145728 | tf_op jit(solution)/shard_map/partial/pallas_call | solution.py:66
  13.5 3.9 %collective-permute-start.13 = (bf16[288,512]{1,0:T(8,128)(2,1)S(1)}, bf16[288,512]{1,0:T(8,128)(2,1)S(1)}, u32[]{:S(2)}, u32[]{:S(2)}) collective-permute-start(bf16[288,512]{1,0:T(8,128)(2,1)S(1)} %fusion.2), channel_id=1, source_target_pairs={{0,32},{8,104},{16,48},{24,120},{32,64},{40,8},{48,80},{56,24},{64... | collective-permute-start | bytes 884744 | tf_op jit(solution)/shard_map/ppermute | solution.py:31
  17.4 1.1 fusion
  19.8 6.0 %partial.7 = (bf16[1024,512]{1,0:T(8,128)(2,1)S(1)}, f32[1024,512]{1,0:T(8,128)S(1)}) custom-call(s32[7]{0:T(128)S(1)} %stack.31.place_ref, bf16[1024,4096]{1,0:T(8,128)(2,1)} %refs_1_.9, bf16[1024,4096]{1,0:T(8,128)(2,1)} %refs_1_.9, bf16[1024,1024]{1,0:T(8,128)(2,1)} %refs_3_.5, bf16[1024,1024]{1,0:T(8,128)(2,1)} %refs_3_.5), custom_call_target="tpu_custom_call" | custom-call | flops 8589934592 | bytes 25165824 | tf_op jit(solution)/shard_map/partial/pallas_call | solution.py:66
  25.9 1.5 %collective-permute-start.4 = (bf16[1024,512]{1,0:T(8,128)(2,1)S(1)}, bf16[1024,512]{1,0:T(8,128)(2,1)S(1)}, u32[]{:S(2)}, u32[]{:S(2)}) collective-permute-start(bf16[1024,512]{1,0:T(8,128)(2,1)S(1)} %get-tuple-element.20), channel_id=1, source_target_pairs={{0,8},{8,0},{16,24},{24,16},{32,40},{40,32},{48,56},{56,48},{64,72... | collective-permute-start | bytes 3145736 | tf_op jit(solution)/shard_map/ppermute | solution.py:22
  27.4 2.3 %collective-permute-start.15 = (bf16[1024,512]{1,0:T(8,128)(2,1)}, bf16[1024,512]{1,0:T(8,128)(2,1)S(1)}, u32[]{:S(2)}, u32[]{:S(2)}) collective-permute-start(bf16[1024,512]{1,0:T(8,128)(2,1)} %convert_element_type.135), channel_id=1, source_target_pairs={{8,16},{16,8},{40,48},{48,40},{72,80},{80,72},{104,112},{112,104},... | collective-permute-start | bytes 3145736 | tf_op jit(solution)/shard_map/ppermute | solution.py:38
  29.7 6.0 %partial.8 = (bf16[1024,512]{1,0:T(8,128)(2,1)S(1)}, f32[1024,512]{1,0:T(8,128)S(1)}) custom-call(s32[7]{0:T(128)S(1)} %stack.31.place_ref, bf16[1024,4096]{1,0:T(8,128)(2,1)} %refs_1_.9, bf16[1024,4096]{1,0:T(8,128)(2,1)} %refs_1_.9, bf16[1024,1024]{1,0:T(8,128)(2,1)} %refs_3_.5, bf16[1024,1024]{1,0:T(8,128)(2,1)} %refs_3_.5), custom_call_target="tpu_custom_call" | custom-call | flops 8589934592 | bytes 25165824 | tf_op jit(solution)/shard_map/partial/pallas_call | solution.py:66
  35.8 6.0 %partial.9 = (bf16[1024,512]{1,0:T(8,128)(2,1)S(1)}, f32[1024,512]{1,0:T(8,128)S(1)}) custom-call(s32[7]{0:T(128)S(1)} %stack.31.place_ref, bf16[1024,4096]{1,0:T(8,128)(2,1)} %refs_1_.9, bf16[1024,4096]{1,0:T(8,128)(2,1)} %refs_1_.9, bf16[1024,1024]{1,0:T(8,128)(2,1)} %refs_3_.5, bf16[1024,1024]{1,0:T(8,128)(2,1)} %refs_3_.5), custom_call_target="tpu_custom_call" | custom-call | flops 8589934592 | bytes 25165824 | tf_op jit(solution)/shard_map/partial/pallas_call | solution.py:66
  42.7 1.3 %collective-permute-start.2 = (bf16[1024,512]{1,0:T(8,128)(2,1)S(1)}, bf16[1024,512]{1,0:T(8,128)(2,1)S(1)}, u32[]{:S(2)}, u32[]{:S(2)}) collective-permute-start(bf16[1024,512]{1,0:T(8,128)(2,1)S(1)} %get-tuple-element.26), channel_id=1, source_target_pairs={{0,8},{8,0},{16,24},{24,16},{32,40},{40,32},{48,56},{56,48},{64,72... | collective-permute-start | bytes 3145736 | tf_op jit(solution)/shard_map/ppermute | solution.py:22
  44.2 1.4 %collective-permute-start.14 = (bf16[288,512]{1,0:T(8,128)(2,1)S(1)}, bf16[288,512]{1,0:T(8,128)(2,1)S(1)}, u32[]{:S(2)}, u32[]{:S(2)}) collective-permute-start(bf16[288,512]{1,0:T(8,128)(2,1)S(1)} %add_convert_fusion.11), channel_id=1, source_target_pairs={{0,32},{8,104},{16,48},{24,120},{32,64},{40,8},{48,80},{56,24},{64... | collective-permute-start | bytes 884744 | tf_op jit(solution)/shard_map/ppermute | solution.py:31
  45.8 2.7 %collective-permute-done.9 = bf16[352,512]{1,0:T(8,128)(2,1)S(1)} collective-permute-done((bf16[352,512]{1,0:T(8,128)(2,1)S(1)}, bf16[352,512]{1,0:T(8,128)(2,1)S(1)}, u32[]{:S(2)}, u32[]{:S(2)}) %collective-permute-start.9) | collective-permute-done | bytes 360480 | tf_op jit(solution)/shard_map/ppermute | solution.py:31
  48.5 1.7 %collective-permute-start.6 = (bf16[384,512]{1,0:T(8,128)(2,1)S(1)}, bf16[384,512]{1,0:T(8,128)(2,1)S(1)}, u32[]{:S(2)}, u32[]{:S(2)}) collective-permute-start(bf16[384,512]{1,0:T(8,128)(2,1)S(1)} %add_convert_fusion.3), channel_id=1, source_target_pairs={{0,32},{8,104},{16,48},{24,120},{32,64},{40,8},{48,80},{56,24},{64... | collective-permute-start | bytes 1179656 | tf_op jit(solution)/shard_map/ppermute | solution.py:31
  50.5 1.2 collective-permute-done.14
  51.8 1.8 %collective-permute-start.16 = (bf16[288,512]{1,0:T(8,128)(2,1)S(1)}, bf16[288,512]{1,0:T(8,128)(2,1)S(1)}, u32[]{:S(2)}, u32[]{:S(2)}) collective-permute-start(bf16[288,512]{1,0:T(8,128)(2,1)S(1)} %add_convert_fusion.10), channel_id=1, source_target_pairs={{0,32},{8,104},{16,48},{24,120},{32,64},{40,8},{48,80},{56,24},{64... | collective-permute-start | bytes 884744 | tf_op jit(solution)/shard_map/ppermute | solution.py:31
  53.6 2.3 %collective-permute-done.6 = bf16[384,512]{1,0:T(8,128)(2,1)S(1)} collective-permute-done((bf16[384,512]{1,0:T(8,128)(2,1)S(1)}, bf16[384,512]{1,0:T(8,128)(2,1)S(1)}, u32[]{:S(2)}, u32[]{:S(2)}) %collective-permute-start.6) | collective-permute-done | bytes 393248 | tf_op jit(solution)/shard_map/ppermute | solution.py:31
  56.1 2.2 %collective-permute-start.7 = (bf16[384,512]{1,0:T(8,128)(2,1)S(1)}, bf16[384,512]{1,0:T(8,128)(2,1)S(1)}, u32[]{:S(2)}, u32[]{:S(2)}) collective-permute-start(bf16[384,512]{1,0:T(8,128)(2,1)S(1)} %add_convert_fusion.2), channel_id=1, source_target_pairs={{0,32},{8,104},{16,48},{24,120},{32,64},{40,8},{48,80},{56,24},{64... | collective-permute-start | bytes 1179656 | tf_op jit(solution)/shard_map/ppermute | solution.py:31
  58.3 1.4 %collective-permute-done.10 = bf16[352,512]{1,0:T(8,128)(2,1)S(1)} collective-permute-done((bf16[352,512]{1,0:T(8,128)(2,1)S(1)}, bf16[352,512]{1,0:T(8,128)(2,1)S(1)}, u32[]{:S(2)}, u32[]{:S(2)}) %collective-permute-start.10) | collective-permute-done | bytes 360480 | tf_op jit(solution)/shard_map/ppermute | solution.py:31
  59.9 2.2 %collective-permute-start.11 = (bf16[352,512]{1,0:T(8,128)(2,1)S(1)}, bf16[352,512]{1,0:T(8,128)(2,1)S(1)}, u32[]{:S(2)}, u32[]{:S(2)}) collective-permute-start(bf16[352,512]{1,0:T(8,128)(2,1)S(1)} %add_convert_fusion.6), channel_id=1, source_target_pairs={{0,32},{8,104},{16,48},{24,120},{32,64},{40,8},{48,80},{56,24},{64... | collective-permute-start | bytes 1081352 | tf_op jit(solution)/shard_map/ppermute | solution.py:31
  63.0 1.5 %collective-permute-start.17 = (bf16[288,512]{1,0:T(8,128)(2,1)S(1)}, bf16[288,512]{1,0:T(8,128)(2,1)S(1)}, u32[]{:S(2)}, u32[]{:S(2)}) collective-permute-start(bf16[288,512]{1,0:T(8,128)(2,1)S(1)} %add_convert_fusion.9), channel_id=1, source_target_pairs={{0,16},{16,0},{8,24},{24,8},{32,48},{48,32},{40,56},{56,40},{64,80... | collective-permute-start | bytes 884744 | tf_op jit(solution)/shard_map/ppermute | solution.py:22
  64.6 2.5 %collective-permute-done.7 = bf16[384,512]{1,0:T(8,128)(2,1)S(1)} collective-permute-done((bf16[384,512]{1,0:T(8,128)(2,1)S(1)}, bf16[384,512]{1,0:T(8,128)(2,1)S(1)}, u32[]{:S(2)}, u32[]{:S(2)}) %collective-permute-start.7) | collective-permute-done | bytes 393248 | tf_op jit(solution)/shard_map/ppermute | solution.py:31
  67.3 1.5 %collective-permute-start.8 = (bf16[384,512]{1,0:T(8,128)(2,1)S(1)}, bf16[384,512]{1,0:T(8,128)(2,1)S(1)}, u32[]{:S(2)}, u32[]{:S(2)}) collective-permute-start(bf16[384,512]{1,0:T(8,128)(2,1)S(1)} %add_convert_fusion.1), channel_id=1, source_target_pairs={{0,16},{16,0},{8,24},{24,8},{32,48},{48,32},{40,56},{56,40},{64,80... | collective-permute-start | bytes 1179656 | tf_op jit(solution)/shard_map/ppermute | solution.py:22
  68.8 2.1 %collective-permute-done.11 = bf16[352,512]{1,0:T(8,128)(2,1)S(1)} collective-permute-done((bf16[352,512]{1,0:T(8,128)(2,1)S(1)}, bf16[352,512]{1,0:T(8,128)(2,1)S(1)}, u32[]{:S(2)}, u32[]{:S(2)}) %collective-permute-start.11) | collective-permute-done | bytes 360480 | tf_op jit(solution)/shard_map/ppermute | solution.py:31
  71.1 1.5 %collective-permute-start.12 = (bf16[352,512]{1,0:T(8,128)(2,1)S(1)}, bf16[352,512]{1,0:T(8,128)(2,1)S(1)}, u32[]{:S(2)}, u32[]{:S(2)}) collective-permute-start(bf16[352,512]{1,0:T(8,128)(2,1)S(1)} %add_convert_fusion.5), channel_id=1, source_target_pairs={{0,16},{16,0},{8,24},{24,8},{32,48},{48,32},{40,56},{56,40},{64,80... | collective-permute-start | bytes 1081352 | tf_op jit(solution)/shard_map/ppermute | solution.py:22
  72.8 4.5 %collective-permute-start.20 = (bf16[288,512]{1,0:T(8,128)(2,1)S(1)}, bf16[288,512]{1,0:T(8,128)(2,1)S(1)}, u32[]{:S(2)}, u32[]{:S(2)}) collective-permute-start(bf16[288,512]{1,0:T(8,128)(2,1)S(1)} %add_convert_fusion.8.refs_2_), channel_id=1, source_target_pairs={{0,8},{8,0},{16,24},{24,16},{32,40},{40,32},{48,56},{56,48},{64,72... | collective-permute-start | bytes 884744 | tf_op jit(solution)/shard_map/ppermute | solution.py:22
  78.4 7.3 %collective-permute-start.18 = (bf16[384,512]{1,0:T(8,128)(2,1)S(1)}, bf16[384,512]{1,0:T(8,128)(2,1)S(1)}, u32[]{:S(2)}, u32[]{:S(2)}) collective-permute-start(bf16[384,512]{1,0:T(8,128)(2,1)S(1)} %add_convert_fusion.refs_0_), channel_id=1, source_target_pairs={{0,8},{8,0},{16,24},{24,16},{32,40},{40,32},{48,56},{56,48},{64,72... | collective-permute-start | bytes 1179656 | tf_op jit(solution)/shard_map/ppermute | solution.py:22
  86.1 3.9 %collective-permute-start.19 = (bf16[352,512]{1,0:T(8,128)(2,1)S(1)}, bf16[352,512]{1,0:T(8,128)(2,1)S(1)}, u32[]{:S(2)}, u32[]{:S(2)}) collective-permute-start(bf16[352,512]{1,0:T(8,128)(2,1)S(1)} %add_convert_fusion.4.refs_1_), channel_id=1, source_target_pairs={{0,8},{8,0},{16,24},{24,16},{32,40},{40,32},{48,56},{56,48},{64,72... | collective-permute-start | bytes 1081352 | tf_op jit(solution)/shard_map/ppermute | solution.py:22
  90.0 1.5 %broadcast_select_fusion.1 = (bf16[1024,512]{1,0:T(8,128)(2,1)S(1)}, bf16[1024,512]{1,0:T(8,128)(2,1)S(1)}) fusion(bf16[1024,512]{1,0:T(8,128)(2,1)} %collective-permute-done.1, pred[]{:T(512)S(6)} %lt.36, bf16[1024,512]{1,0:T(8,128)(2,1)S(1)} %collective-permute-done.15, pred[]{:T(512)S(6)} %or.3, f32[1024,512]{1,0:T(8,128)S(1)} %bitcast.10), kind=kLoop, calls=%fused_computation.1 | loop fusion | flops 2097152 | bytes 6291458 | tf_op jit(solution)/shard_map/jit(_where)/select_n | solution.py:133
  91.5 20.6 %root.1 = (bf16[1024,1024]{1,0:T(8,128)(2,1)S(1)}, bf16[1024,512]{1,0:T(8,128)(2,1)S(1)}, bf16[1024,512]{1,0:T(8,128)(2,1)S(1)}) custom-call(s32[7]{0:T(128)S(1)} %stack.31.place_ref, bf16[384,512]{1,0:T(8,128)(2,1)S(1)} %add_convert_fusion.refs_0_, bf16[352,512]{1,0:T(8,128)(2,1)S(1)} %add_convert_fusion.4.refs_1_, ...), custom_call_target="tpu_custom_call" | custom-call | flops 17179869184 | bytes 8388608 | tf_op jit(solution)/shard_map/root/pallas_call | solution.py:294
  112.3 3.2 %statistics.1 = f32[1024,512]{1,0:T(8,128)} custom-call(s32[7]{0:T(128)S(1)} %stack.31.place_ref, bf16[1024,512]{1,0:T(8,128)(2,1)S(1)} %get-tuple-element.31.own_ref, bf16[1024,512]{1,0:T(8,128)(2,1)S(1)} %get-tuple-element.32.mate_ref, f32[1024,512]{1,0:T(8,128)S(1)} %bitcast.11), custom_call_target="tpu_custom_call" | custom-call | flops 1073741824 | bytes 6291456 | tf_op jit(solution)/shard_map/statistics/pallas_call | solution.py:305
  116.3 2.7 %update.1 = bf16[256,1024]{1,0:T(8,128)(2,1)} custom-call(s32[7]{0:T(128)S(1)} %stack.31.place_ref, bf16[1024,512]{1,0:T(8,128)(2,1)S(1)} %get-tuple-element.31.own_ref, bf16[1024,512]{1,0:T(8,128)(2,1)S(1)} %get-tuple-element.32.mate_ref, bf16[1024,1024]{1,0:T(8,128)(2,1)S(1)} %get-tuple-element.33.own_root_ref, ...), custom_call_target="tpu_custom_call" | custom-call | flops 1073741824 | bytes 8388608 | tf_op jit(solution)/shard_map/update/pallas_call | solution.py:314
  (40 shorter events, 9.6 us)
Async XLA Ops:
  0.8 6.1 %copy-start = (f32[1,1,1024,512]{3,2,1,0:T(8,128)S(1)}, f32[1,1,1024,512]{3,2,1,0:T(8,128)}, u32[]{:S(2)}) copy-start(f32[1,1,1024,512]{3,2,1,0:T(8,128)} %param.5) | copy-start | bytes 6291460
  5.4 7.1 %collective-permute-start = (bf16[1024,512]{1,0:T(8,128)(2,1)S(1)}, bf16[1024,512]{1,0:T(8,128)(2,1)}, u32[]{:S(2)}, u32[]{:S(2)}) collective-permute-start(bf16[1024,512]{1,0:T(8,128)(2,1)S(1)} %partial.5), channel_id=1, source_target_pairs={{0,8},{8,0},{16,24},{24,16},{32,40},{40,32},{48,56},{56,48},{64,72... | collective-permute-start | bytes 3145736 | tf_op jit(solution)/shard_map/ppermute | solution.py:22
  8.0 19.4 %collective-permute-start.1 = (bf16[1024,512]{1,0:T(8,128)(2,1)}, bf16[1024,512]{1,0:T(8,128)(2,1)}, u32[]{:S(2)}, u32[]{:S(2)}) collective-permute-start(bf16[1024,512]{1,0:T(8,128)(2,1)} %convert_element_type.135), channel_id=1, source_target_pairs={{0,16},{24,8},{8,0},{16,24},{32,48},{56,40},{40,32},{48,56},{64,80... | collective-permute-start | bytes 3145736 | tf_op jit(solution)/shard_map/ppermute | solution.py:38
  13.5 28.3 %collective-permute-start.13 = (bf16[288,512]{1,0:T(8,128)(2,1)S(1)}, bf16[288,512]{1,0:T(8,128)(2,1)S(1)}, u32[]{:S(2)}, u32[]{:S(2)}) collective-permute-start(bf16[288,512]{1,0:T(8,128)(2,1)S(1)} %fusion.2), channel_id=1, source_target_pairs={{0,32},{8,104},{16,48},{24,120},{32,64},{40,8},{48,80},{56,24},{64... | collective-permute-start | bytes 884744 | tf_op jit(solution)/shard_map/ppermute | solution.py:31
  18.6 25.6 %collective-permute-start.5 = (bf16[384,512]{1,0:T(8,128)(2,1)S(1)}, bf16[384,512]{1,0:T(8,128)(2,1)S(1)}, u32[]{:S(2)}, u32[]{:S(2)}) collective-permute-start(bf16[384,512]{1,0:T(8,128)(2,1)S(1)} %fusion), channel_id=1, source_target_pairs={{0,32},{8,104},{16,48},{24,120},{32,64},{40,8},{48,80},{56,24},{64... | collective-permute-start | bytes 1179656 | tf_op jit(solution)/shard_map/ppermute | solution.py:31
  25.9 16.8 %collective-permute-start.4 = (bf16[1024,512]{1,0:T(8,128)(2,1)S(1)}, bf16[1024,512]{1,0:T(8,128)(2,1)S(1)}, u32[]{:S(2)}, u32[]{:S(2)}) collective-permute-start(bf16[1024,512]{1,0:T(8,128)(2,1)S(1)} %get-tuple-element.20), channel_id=1, source_target_pairs={{0,8},{8,0},{16,24},{24,16},{32,40},{40,32},{48,56},{56,48},{64,72... | collective-permute-start | bytes 3145736 | tf_op jit(solution)/shard_map/ppermute | solution.py:22
  27.4 23.0 %collective-permute-start.15 = (bf16[1024,512]{1,0:T(8,128)(2,1)}, bf16[1024,512]{1,0:T(8,128)(2,1)S(1)}, u32[]{:S(2)}, u32[]{:S(2)}) collective-permute-start(bf16[1024,512]{1,0:T(8,128)(2,1)} %convert_element_type.135), channel_id=1, source_target_pairs={{8,16},{16,8},{40,48},{48,40},{72,80},{80,72},{104,112},{112,104},... | collective-permute-start | bytes 3145736 | tf_op jit(solution)/shard_map/ppermute | solution.py:38
  35.7 15.9 %collective-permute-start.3 = (bf16[1024,512]{1,0:T(8,128)(2,1)S(1)}, bf16[1024,512]{1,0:T(8,128)(2,1)S(1)}, u32[]{:S(2)}, u32[]{:S(2)}) collective-permute-start(bf16[1024,512]{1,0:T(8,128)(2,1)S(1)} %get-tuple-element.22), channel_id=1, source_target_pairs={{0,8},{8,0},{16,24},{24,16},{32,40},{40,32},{48,56},{56,48},{64,72... | collective-permute-start | bytes 3145736 | tf_op jit(solution)/shard_map/ppermute | solution.py:22
  41.8 6.6 %collective-permute-start.9 = (bf16[352,512]{1,0:T(8,128)(2,1)S(1)}, bf16[352,512]{1,0:T(8,128)(2,1)S(1)}, u32[]{:S(2)}, u32[]{:S(2)}) collective-permute-start(bf16[352,512]{1,0:T(8,128)(2,1)S(1)} %fusion.1), channel_id=1, source_target_pairs={{0,32},{8,104},{16,48},{24,120},{32,64},{40,8},{48,80},{56,24},{64... | collective-permute-start | bytes 1081352 | tf_op jit(solution)/shard_map/ppermute | solution.py:31
  42.7 19.4 %collective-permute-start.2 = (bf16[1024,512]{1,0:T(8,128)(2,1)S(1)}, bf16[1024,512]{1,0:T(8,128)(2,1)S(1)}, u32[]{:S(2)}, u32[]{:S(2)}) collective-permute-start(bf16[1024,512]{1,0:T(8,128)(2,1)S(1)} %get-tuple-element.26), channel_id=1, source_target_pairs={{0,8},{8,0},{16,24},{24,16},{32,40},{40,32},{48,56},{56,48},{64,72... | collective-permute-start | bytes 3145736 | tf_op jit(solution)/shard_map/ppermute | solution.py:22
  44.2 7.5 %collective-permute-start.14 = (bf16[288,512]{1,0:T(8,128)(2,1)S(1)}, bf16[288,512]{1,0:T(8,128)(2,1)S(1)}, u32[]{:S(2)}, u32[]{:S(2)}) collective-permute-start(bf16[288,512]{1,0:T(8,128)(2,1)S(1)} %add_convert_fusion.11), channel_id=1, source_target_pairs={{0,32},{8,104},{16,48},{24,120},{32,64},{40,8},{48,80},{56,24},{64... | collective-permute-start | bytes 884744 | tf_op jit(solution)/shard_map/ppermute | solution.py:31
  48.5 7.4 %collective-permute-start.6 = (bf16[384,512]{1,0:T(8,128)(2,1)S(1)}, bf16[384,512]{1,0:T(8,128)(2,1)S(1)}, u32[]{:S(2)}, u32[]{:S(2)}) collective-permute-start(bf16[384,512]{1,0:T(8,128)(2,1)S(1)} %add_convert_fusion.3), channel_id=1, source_target_pairs={{0,32},{8,104},{16,48},{24,120},{32,64},{40,8},{48,80},{56,24},{64... | collective-permute-start | bytes 1179656 | tf_op jit(solution)/shard_map/ppermute | solution.py:31
  50.4 9.3 %collective-permute-start.10 = (bf16[352,512]{1,0:T(8,128)(2,1)S(1)}, bf16[352,512]{1,0:T(8,128)(2,1)S(1)}, u32[]{:S(2)}, u32[]{:S(2)}) collective-permute-start(bf16[352,512]{1,0:T(8,128)(2,1)S(1)} %add_convert_fusion.7), channel_id=1, source_target_pairs={{0,32},{8,104},{16,48},{24,120},{32,64},{40,8},{48,80},{56,24},{64... | collective-permute-start | bytes 1081352 | tf_op jit(solution)/shard_map/ppermute | solution.py:31
  51.8 11.1 %collective-permute-start.16 = (bf16[288,512]{1,0:T(8,128)(2,1)S(1)}, bf16[288,512]{1,0:T(8,128)(2,1)S(1)}, u32[]{:S(2)}, u32[]{:S(2)}) collective-permute-start(bf16[288,512]{1,0:T(8,128)(2,1)S(1)} %add_convert_fusion.10), channel_id=1, source_target_pairs={{0,32},{8,104},{16,48},{24,120},{32,64},{40,8},{48,80},{56,24},{64... | collective-permute-start | bytes 884744 | tf_op jit(solution)/shard_map/ppermute | solution.py:31
  56.1 11.0 %collective-permute-start.7 = (bf16[384,512]{1,0:T(8,128)(2,1)S(1)}, bf16[384,512]{1,0:T(8,128)(2,1)S(1)}, u32[]{:S(2)}, u32[]{:S(2)}) collective-permute-start(bf16[384,512]{1,0:T(8,128)(2,1)S(1)} %add_convert_fusion.2), channel_id=1, source_target_pairs={{0,32},{8,104},{16,48},{24,120},{32,64},{40,8},{48,80},{56,24},{64... | collective-permute-start | bytes 1179656 | tf_op jit(solution)/shard_map/ppermute | solution.py:31
  59.9 11.0 %collective-permute-start.11 = (bf16[352,512]{1,0:T(8,128)(2,1)S(1)}, bf16[352,512]{1,0:T(8,128)(2,1)S(1)}, u32[]{:S(2)}, u32[]{:S(2)}) collective-permute-start(bf16[352,512]{1,0:T(8,128)(2,1)S(1)} %add_convert_fusion.6), channel_id=1, source_target_pairs={{0,32},{8,104},{16,48},{24,120},{32,64},{40,8},{48,80},{56,24},{64... | collective-permute-start | bytes 1081352 | tf_op jit(solution)/shard_map/ppermute | solution.py:31
  63.0 9.6 %collective-permute-start.17 = (bf16[288,512]{1,0:T(8,128)(2,1)S(1)}, bf16[288,512]{1,0:T(8,128)(2,1)S(1)}, u32[]{:S(2)}, u32[]{:S(2)}) collective-permute-start(bf16[288,512]{1,0:T(8,128)(2,1)S(1)} %add_convert_fusion.9), channel_id=1, source_target_pairs={{0,16},{16,0},{8,24},{24,8},{32,48},{48,32},{40,56},{56,40},{64,80... | collective-permute-start | bytes 884744 | tf_op jit(solution)/shard_map/ppermute | solution.py:22
  67.3 11.0 %collective-permute-start.8 = (bf16[384,512]{1,0:T(8,128)(2,1)S(1)}, bf16[384,512]{1,0:T(8,128)(2,1)S(1)}, u32[]{:S(2)}, u32[]{:S(2)}) collective-permute-start(bf16[384,512]{1,0:T(8,128)(2,1)S(1)} %add_convert_fusion.1), channel_id=1, source_target_pairs={{0,16},{16,0},{8,24},{24,8},{32,48},{48,32},{40,56},{56,40},{64,80... | collective-permute-start | bytes 1179656 | tf_op jit(solution)/shard_map/ppermute | solution.py:22
  71.1 14.8 %collective-permute-start.12 = (bf16[352,512]{1,0:T(8,128)(2,1)S(1)}, bf16[352,512]{1,0:T(8,128)(2,1)S(1)}, u32[]{:S(2)}, u32[]{:S(2)}) collective-permute-start(bf16[352,512]{1,0:T(8,128)(2,1)S(1)} %add_convert_fusion.5), channel_id=1, source_target_pairs={{0,16},{16,0},{8,24},{24,8},{32,48},{48,32},{40,56},{56,40},{64,80... | collective-permute-start | bytes 1081352 | tf_op jit(solution)/shard_map/ppermute | solution.py:22
  72.8 18.7 %collective-permute-start.20 = (bf16[288,512]{1,0:T(8,128)(2,1)S(1)}, bf16[288,512]{1,0:T(8,128)(2,1)S(1)}, u32[]{:S(2)}, u32[]{:S(2)}) collective-permute-start(bf16[288,512]{1,0:T(8,128)(2,1)S(1)} %add_convert_fusion.8.refs_2_), channel_id=1, source_target_pairs={{0,8},{8,0},{16,24},{24,16},{32,40},{40,32},{48,56},{56,48},{64,72... | collective-permute-start | bytes 884744 | tf_op jit(solution)/shard_map/ppermute | solution.py:22
  78.4 13.1 %collective-permute-start.18 = (bf16[384,512]{1,0:T(8,128)(2,1)S(1)}, bf16[384,512]{1,0:T(8,128)(2,1)S(1)}, u32[]{:S(2)}, u32[]{:S(2)}) collective-permute-start(bf16[384,512]{1,0:T(8,128)(2,1)S(1)} %add_convert_fusion.refs_0_), channel_id=1, source_target_pairs={{0,8},{8,0},{16,24},{24,16},{32,40},{40,32},{48,56},{56,48},{64,72... | collective-permute-start | bytes 1179656 | tf_op jit(solution)/shard_map/ppermute | solution.py:22
  86.1 5.4 %collective-permute-start.19 = (bf16[352,512]{1,0:T(8,128)(2,1)S(1)}, bf16[352,512]{1,0:T(8,128)(2,1)S(1)}, u32[]{:S(2)}, u32[]{:S(2)}) collective-permute-start(bf16[352,512]{1,0:T(8,128)(2,1)S(1)} %add_convert_fusion.4.refs_1_), channel_id=1, source_target_pairs={{0,8},{8,0},{16,24},{24,16},{32,40},{40,32},{48,56},{56,48},{64,72... | collective-permute-start | bytes 1081352 | tf_op jit(solution)/shard_map/ppermute | solution.py:22
  112.1 4.2 %collective-permute-start.21 = (bf16[1024,1024]{1,0:T(8,128)(2,1)S(1)}, bf16[1024,1024]{1,0:T(8,128)(2,1)S(1)}, u32[]{:S(2)}, u32[]{:S(2)}) collective-permute-start(bf16[1024,1024]{1,0:T(8,128)(2,1)S(1)} %get-tuple-element.33.own_root_ref), channel_id=1, source_target_pairs={{0,8},{8,0},{16,24},{24,16},{32,40},{40,32},{48,56},{56,48},{64,72... | collective-permute-start | bytes 6291464 | tf_op jit(solution)/shard_map/ppermute | solution.py:22
